TPU v7x, 32 devices: a whole 2x2x4 slice. The times are simulated.
32 devices in a mesh: grp: 2 (over y), src: 4 (over z), chan: 2 (over x), row: 2 (over core).
Axes of the slice: x: 2, y: 2, z: 4, core: 2. Of those that a mesh axis runs over, the one named last changes fastest.
Arguments:
- features: bfloat16 [64, 128, 512], P('chan', ('grp', 'row'), 'src'), parts along dimension 1, may hold values from -6 to 6
- layout: int32 [128, 512], P(('grp', 'row'), 'chan'), parts along dimension 0, may hold values 0 or 1
- conv_weight: bfloat16 [4, 4, 9, 64, 64], P('src'), may hold values from -0.25 to 0.25
- conv_bias: float32 [4, 4, 64], P('src'), may hold values from -2 to 2
- head_weight: bfloat16 [4, 64, 16], P('src'), may hold values from -0.75 to 0.75
- transmission: float32 [4, 16], P('src'), may hold values from -3 to 3
- point_weight: float32 [128], replicated, may hold values from 0.1 to 1
- assignment: int32 [128, 1], replicated, may hold values from 0 to 3
Outputs:
- intensity: float32 [8, 4, 32, 512], P(None, ('grp', 'row'), 'src', 'chan'), parts along dimension 1
There are 2 independent parts, one for each index of `grp`. A program takes and returns all parts, laid end to end along the dimension named above; an argument that names none is the same for every part. Nothing has to cross between parts.
Inputs may be any that keep to these rules, and one draw needn't show every extreme that they name: `assignment`: every cluster is named by at least one point.
All inputs are finite; a program needn't handle non-finite values. No bound on the sum of `layout` on one device may be relied on, other than what follows from the above.
Results may differ from a plain program's by a relative error of at most 0.009.
Values may be sent and summed in bfloat16 or wider, within the bound.
A program may use at most 64 MiB of HBM per device.

v0:
```python
import functools
import math

import jax
import jax.numpy as jnp
from jax import lax
from jax.experimental import pallas as pl
from jax.experimental.pallas import tpu as pltpu
from jax.sharding import PartitionSpec as P


def with_halo(block, sides, width):
    for axis, dim in sides:
        count = lax.axis_size(axis)
        forward = [(i, i + 1) for i in range(count - 1)]
        backward = [(target, source) for source, target in forward]
        low = lax.ppermute(
            lax.slice_in_dim(block, block.shape[dim] - width, None, axis=dim), axis, forward
        )
        high = lax.ppermute(lax.slice_in_dim(block, 0, width, axis=dim), axis, backward)
        block = jnp.concatenate([low, block, high], axis=dim)
    return block


def advance(core_cells, padded, weights, biases, dilation):
    tile_rows, tile_cols = (core_cells.shape[1], core_cells.shape[2])
    kernel = weights.reshape(3, 3, weights.shape[1], weights.shape[2])
    window = padded[:, : tile_rows + 2 * dilation, : tile_cols + 2 * dilation]
    summed = lax.conv_general_dilated(
        window[None],
        kernel,
        (1, 1),
        "VALID",
        rhs_dilation=(dilation, dilation),
        dimension_numbers=("NCHW", "HWIO", "NCHW"),
        preferred_element_type=jnp.float32,
    )[0]
    summed = summed + biases[:, None, None]
    return (core_cells.astype(jnp.float32) + jax.nn.gelu(summed, approximate=True)).astype(
        jnp.bfloat16
    )


def by_cluster(
    features, layout, conv_weight, conv_bias, head_weight, transmission, point_weight, assignment
):
    channels = lax.all_gather(features, "chan", axis=0, tiled=True)
    full_cache = lax.all_gather(channels, "src", axis=2, tiled=True)
    column_width = full_cache.shape[2] // lax.axis_size("chan")
    tile_cache = lax.dynamic_slice_in_dim(
        full_cache, lax.axis_index("chan") * column_width, column_width, 2
    )
    weights = conv_weight[0]
    biases = conv_bias[0]
    hidden = tile_cache
    for layer_index in range(weights.shape[0]):
        dilation = 2**layer_index
        padded = with_halo(hidden, (("chan", 2), ("row", 1)), dilation)
        hidden = advance(hidden, padded, weights[layer_index], biases[layer_index], dilation)
    field_map = jnp.einsum(
        "ihw,ik->khw", hidden, head_weight[0], preferred_element_type=jnp.float32
    )
    field_map = field_map + layout.astype(jnp.float32)[None] * transmission[0][:, None, None]
    planes = field_map.shape[0] // 2
    power_map = field_map[:planes] ** 2 + field_map[planes:] ** 2
    chosen = assignment[:, 0] == lax.axis_index("src")
    cluster_share = jnp.sum(jnp.where(chosen, point_weight, jnp.zeros((), jnp.float32))) / jnp.sum(
        point_weight
    )
    summed = lax.psum_scatter(
        (power_map * cluster_share).astype(jnp.bfloat16), "src", scatter_dimension=1, tiled=True
    ).astype(jnp.float32)
    return summed[:, None]


def gelu(v):
    c = math.sqrt(2.0 / math.pi)
    return 0.5 * v * (1.0 + jnp.tanh(v * (c + (c * 0.044715) * (v * v))))


def beside(h, d):
    n = h.shape[1]
    sub = lax.broadcasted_iota(jnp.int32, h.shape, 1)
    low = lax.broadcasted_iota(jnp.int32, h.shape, 2) < h.shape[2] // 2
    rolled = jnp.where(low, pltpu.roll(h, n - d, 1), pltpu.roll(h, d, 1))
    keep = jnp.where(low, sub, n - 1 - sub) < n - d
    return jnp.where(keep, rolled, 0.0)


def repair(h, d):
    shape = h.shape
    h = h.reshape(-1, 8, shape[2])
    sub = lax.broadcasted_iota(jnp.int32, h.shape, 1)
    half = lax.broadcasted_iota(jnp.int32, h.shape, 2) // (shape[2] // 2)
    bit = (sub // d) % 2
    other = pltpu.roll(h, shape[2] // 2, 2)
    swapped = jnp.where(bit == 1, pltpu.roll(other, d, 1), pltpu.roll(other, 8 - d, 1))
    return jnp.where(bit == half, h, swapped).reshape(shape)


def chunks_of(groups, d, rows):
    best = 1
    for g in range(1, groups + 1):
        if groups % g == 0 and g * d * rows <= 512:
            best = g
    return best


MESH = pl.DeviceIdType.MESH


def xor(s, k):
    total = s
    bit = 1
    while bit <= k:
        if k & bit:
            total = total + bit - 2 * bit * ((s // bit) % 2)
        bit *= 2
    return total


def pixel_kernel(
    layers, n_src, width, t_ref, w_ref, p_ref, m_ref, pw_ref, as_ref, o_ref, *scratch
):
    bufs = scratch[: layers + 1]
    got, wraw, pbuf, mbuf, wide, acc, obuf = scratch[layers + 1 : layers + 8]
    fs, fr, es, er, ws, wr, vs, vr, ps, pr, ms, mr, os, orr, lw, lp = scratch[layers + 8 :]
    s, c, r = (lax.axis_index(a) for a in ("src", "chan", "row"))
    halo = 2**layers - 1
    lanes = t_ref.shape[2]
    half_rows = t_ref.shape[1]
    rows = 2 * half_rows
    piece = t_ref.shape[0] // 8
    here = 2 * c + r
    side = c

    barrier = pltpu.get_barrier_semaphore()
    for s1 in range(n_src):
        for c1 in range(2):
            for r1 in range(2):
                @pl.when(jnp.logical_not((s == s1) & (c == c1) & (r == r1)))
                def _():
                    pl.semaphore_signal(
                        barrier, inc=1, device_id={"src": s1, "chan": c1, "row": r1},
                        device_id_type=MESH,
                    )
    pl.semaphore_wait(barrier, 4 * n_src - 1)

    def remote(src, dst, a, b, s1, c1, r1):
        return pltpu.make_async_remote_copy(
            src_ref=src, dst_ref=dst, send_sem=a, recv_sem=b,
            device_id={"src": s1, "chan": c1, "row": r1}, device_id_type=MESH,
        )

    def main_copy(c1, r1):
        return (
            t_ref.at[pl.ds(piece * (3 * c1 + 2 * r1), 3 * piece)],
            got.at[here, pl.ds(piece * (1 - c1), 3 * piece)],
        )

    def edge_copy(c1, r1):
        at = 7 * (1 - c1) if c1 == r1 else 1 + 5 * c1
        return t_ref.at[pl.ds(piece * at, piece)], got.at[here, pl.ds(piece * 3 * c1, piece)]

    def each(act):
        for c1 in (0, 1):
            for r1 in (0, 1):
                k = 2 * c1 + r1
                me = (c == c1) & (r == r1)
                act(c1, r1, k, me)

    def send_main(c1, r1, k, me):
        src, dst = main_copy(c1, r1)
        pl.when(jnp.logical_not(me))(
            lambda: remote(src, dst, fs.at[k], fr.at[here], s, c1, r1).start())
        pl.when(me)(lambda: pltpu.make_async_copy(src, dst, fr.at[here]).start())

    def edge_step(c1):
        return 1 - 2 * c1

    def send_edge(c1, r1, k, me):
        src, dst = edge_copy(c1, r1)
        if c1 == r1:
            s1 = s + edge_step(c1)
            pl.when((s1 >= 0) & (s1 < n_src))(
                lambda: remote(src, dst, es.at[k], er.at[here], s1, c1, r1).start())
        else:
            pl.when(jnp.logical_not(me))(
                lambda: remote(src, dst, es.at[k], er.at[here], s, c1, r1).start())
            pl.when(me)(lambda: pltpu.make_async_copy(src, dst, er.at[here]).start())

    def send_mask(c1, r1, k, me):
        src, dst = m_ref.at[k], mbuf.at[r]
        owner = c == (2 * s) // n_src
        pl.when(owner & jnp.logical_not(me))(
            lambda: remote(src, dst, ms.at[k], mr.at[r], s, c1, r1).start())
        pl.when(owner & me)(lambda: pltpu.make_async_copy(src, dst, mr.at[r]).start())

    each(send_main)
    each(send_edge)

    def wz(k):
        return remote(w_ref.at[r], wraw.at[k, r], ws.at[k], wr.at[k], xor(s, k), c, r)

    def pz(k):
        return remote(p_ref, pbuf.at[k], ps.at[k], pr.at[k], xor(s, k), c, r)

    for k in range(1, n_src):
        pz(k).start()
        wz(k).start()
    each(send_mask)
    own_w = pltpu.make_async_copy(w_ref, wraw.at[0], lw)
    own_p = pltpu.make_async_copy(p_ref, pbuf.at[0], lp)
    own_w.start()
    own_p.start()

    wide[...] = jnp.zeros_like(wide)
    outside = ((here == 0) & (s == 0)) | ((here == 3) & (s == n_src - 1))

    @pl.when(outside)
    def _():
        for k in range(4):
            got[k, pl.ds(piece * 3 * side, piece)] = jnp.zeros((piece,) + got.shape[2:], got.dtype)

    ch = lanes // 2

    def build(k):
        low = lax.broadcasted_iota(jnp.int32, (ch, lanes), 1) < ch
        per = layers // 2
        for l in range(layers):
            raw = lambda i: wraw[k, l // per, (l % per) * 5 + i].astype(jnp.float32)
            firsts = [raw(b) for b in range(3)]
            q0, q1 = raw(3), raw(4)
            seconds = [q0, pltpu.roll(q0, ch, 1), q1]
            for b in range(3):
                w10, w2 = firsts[b], seconds[b]
                swap = pltpu.roll(w10, ch, 1)
                blocks = [
                    w10,
                    jnp.where(low, w2, swap),
                    jnp.where(low, 0.0, pltpu.roll(w2, ch, 1)),
                    jnp.where(low, swap, 0.0),
                ]
                for j in range(4):
                    v = blocks[j].astype(wide.dtype)
                    for ic in range(2):
                        at = (b + ic) * 4 * ch + j * ch
                        wide[l, at : at + ch, ic * lanes : (ic + 1) * lanes] = v

    own_w.wait()
    own_p.wait()
    build(0)

    def wait_main(c1, r1, k, me):
        src, _ = main_copy(0, 0)
        dst = got.at[k, pl.ds(piece * (1 - side), 3 * piece)]
        pl.when(jnp.logical_not(me))(
            lambda: remote(src, dst, fs.at[k], fr.at[k], s, c1, r1).wait_recv())
        pl.when(me)(lambda: pltpu.make_async_copy(src, dst, fr.at[k]).wait())

    def wait_edge(c1, r1, k, me):
        src, _ = edge_copy(0, 0)
        dst = got.at[k, pl.ds(piece * 3 * side, piece)]
        far = c == r
        inside = jnp.logical_not(outside)
        pl.when(jnp.where(far, inside, jnp.logical_not(me)))(
            lambda: remote(src, dst, es.at[k], er.at[k], s, c1, r1).wait_recv())
        pl.when(jnp.logical_not(far) & me)(
            lambda: pltpu.make_async_copy(src, dst, er.at[k]).wait())

    each(wait_main)
    each(wait_edge)
    n_in = 2 * t_ref.shape[0] // 4 + 2 * halo
    q = ch // 2
    rin = lax.broadcasted_iota(jnp.int32, (2 * lanes, 2 * lanes), 0)
    rout = lax.broadcasted_iota(jnp.int32, (2 * lanes, 2 * lanes), 1)
    want = (rout // q % 2) * lanes + (rout // lanes) * ch + (rout // ch % 2) * q + rout % q
    place = jnp.where(rin == want, 1.0, 0.0).astype(t_ref.dtype)
    strips = []
    for r1 in range(2):
        pairs = got.shape[1]
        lhs = jnp.concatenate(
            [got[2 * c1 + r1].reshape(pairs * half_rows, lanes) for c1 in range(2)], axis=1)
        v = jnp.dot(lhs, place, preferred_element_type=jnp.float32)
        v = v.reshape(pairs, half_rows, 2 * lanes)
        parts = []
        for t in range(pairs):
            parts += [v[t : t + 1, :, :lanes], v[t : t + 1, :, lanes:]]
        skip = (2 * pairs - n_in) // 2
        strips.append(jnp.concatenate(parts[skip : skip + n_in], axis=0))
    x = jnp.concatenate(strips, axis=1)
    bufs[0][:, :, :lanes] = x.astype(jnp.bfloat16)
    bufs[0][:, :, lanes:] = beside(x, 1).astype(jnp.bfloat16)

    own_cols = n_in - 2 * halo
    start = (4 * s + here) * own_cols
    for r1 in range(2):
        for_self = (c == (2 * s) // n_src) & (r == r1)
        pl.when(jnp.logical_not(for_self))(
            lambda: remote(m_ref.at[0], mbuf.at[r1], ms.at[0], mr.at[r1], s, c, r).wait_recv())
        pl.when(for_self)(
            lambda: pltpu.make_async_copy(m_ref.at[0], mbuf.at[r1], mr.at[r1]).wait())

    def share_copy(k):
        return remote(wraw.at[k, r], wraw.at[k, r], vs.at[k], vr.at[k], s, c, 1 - r)

    total = jnp.sum(pw_ref[...], axis=1, keepdims=True)

    def compute(k, cid):
        share = jnp.sum(jnp.where(as_ref[...] == cid, pw_ref[...], 0.0), axis=1, keepdims=True) / total
        margin = 0
        for l in range(layers):
            d = 2**l
            src = bufs[l]
            n_out = src.shape[0] - 2 * d
            margin += d
            groups = n_out // (2 * d)
            per = chunks_of(groups, d, rows)
            bias = pbuf[k, 2 * q2 + l : 2 * q2 + l + 1, :]
            for chunk in range(groups // per):
                base = chunk * per * 2 * d
                lhs = jnp.concatenate(
                    [
                        jnp.concatenate(
                            [src[base + 2 * d * g + j * d : base + 2 * d * g + (j + 1) * d] for g in range(per)],
                            axis=0,
                        ).reshape(per * d * rows, 2 * lanes)
                        for j in range(4)
                    ],
                    axis=1,
                )
                out = jnp.dot(lhs, wide[l], preferred_element_type=jnp.float32)
                out = out.reshape(per * d, rows, 2 * lanes)
                parts = []
                for g in range(per):
                    parts += [out[g * d : (g + 1) * d, :, :lanes], out[g * d : (g + 1) * d, :, lanes:]]
                z = jnp.concatenate(parts, axis=0) + bias[None]
                n = per * 2 * d
                centre = src[base + d : base + d + n, :, :lanes].astype(jnp.float32)
                h = centre + gelu(z)
                col = lax.broadcasted_iota(jnp.int32, h.shape, 0) + (start - halo + margin + base)
                h = jnp.where((col >= 0) & (col < width), h, 0.0)
                h = h.astype(jnp.bfloat16).astype(jnp.float32)
                if l + 1 < layers:
                    h = repair(h, d)
                    bufs[l + 1][base : base + n, :, :lanes] = h.astype(jnp.bfloat16)
                    bufs[l + 1][base : base + n, :, lanes:] = beside(h, 2 * d).astype(jnp.bfloat16)
                else:
                    bufs[l + 1][base * rows : (base + n) * rows] = h.reshape(n * rows, lanes)
        final = bufs[layers]
        head = pbuf[k, : 2 * q2, :]
        low = lax.broadcasted_iota(jnp.int32, head.shape, 1) < ch
        h_lo = jnp.where(low, head, 0.0)
        h_hi = jnp.where(low, 0.0, pltpu.roll(head, ch, 1))
        tcol = head[:, ch : ch + 1]
        hw = jnp.concatenate([h_lo[:q2], h_hi[:q2], h_lo[q2:], h_hi[q2:]], axis=0).astype(jnp.bfloat16)
        tr = jnp.concatenate([tcol[:q2], tcol[:q2], tcol[q2:], tcol[q2:]], axis=0)
        for g in range(rows // 8):
            block = jnp.concatenate(
                [final[pl.ds(g * 8 + b, own_cols, stride=rows), :] for b in range(8)], axis=0
            ).astype(jnp.bfloat16)
            field = lax.dot_general(
                hw, block, (((1,), (1,)), ((), ())), preferred_element_type=jnp.float32)
            m = mbuf[g // 2, 2 * (g % 2) : 2 * (g % 2) + 2]
            mm = jnp.concatenate(
                [jnp.broadcast_to(m[i : i + 1], (q2, m.shape[1])) for i in (0, 1, 0, 1)], axis=0)
            field = field + mm * tr
            power = (field[: 2 * q2] ** 2 + field[2 * q2 :] ** 2) * share
            if k == 0:
                acc[g] = power
            else:
                acc[g] = acc[g] + power

    q2 = acc.shape[1] // 2
    for k in range(n_src):
        if k + 1 < n_src:
            wz(k + 1).wait_recv()
            share_copy(k + 1).start()
        if k > 0:
            remote(
                wraw.at[k, 1 - r], wraw.at[k, 1 - r], vs.at[k], vr.at[k], s, c, 1 - r
            ).wait_recv()
            pz(k).wait_recv()
            build(k)
        compute(k, xor(s, k))

    c2 = (2 * s) // n_src
    slot = 4 * (s % 2) + here

    def outgoing(act):
        for s1 in range(n_src):
            for r1 in range(2):
                k = 2 * s1 + r1
                src = acc.at[2 * r1 + s1 // 2, pl.ds((s1 % 2) * q2, q2)]
                me = (s == s1) & (c == c2) & (r == r1)
                act(s1, r1, k, src, me)

    def send_out(s1, r1, k, src, me):
        dst = obuf.at[slot]
        pl.when(jnp.logical_not(me))(
            lambda: remote(src, dst, os.at[k], orr.at[slot], s1, c2, r1).start())
        pl.when(me)(lambda: pltpu.make_async_copy(src, dst, orr.at[slot]).start())

    outgoing(send_out)
    mine = c == c2
    for k in range(2 * n_src):
        me = mine & (slot == k)
        src = acc.at[0, pl.ds(0, q2)]
        pl.when(jnp.logical_not(me))(
            lambda: remote(src, obuf.at[k], os.at[k], orr.at[k], s, c, r).wait_recv())
        pl.when(me)(lambda: pltpu.make_async_copy(src, obuf.at[k], orr.at[k]).wait())
    for b in range(8):
        o_ref[:, b, :] = jnp.concatenate(
            [obuf[k, :, b * own_cols : (b + 1) * own_cols] for k in range(2 * n_src)], axis=1)

    def sent_main(c1, r1, k, me):
        src, dst = main_copy(c1, r1)
        pl.when(jnp.logical_not(me))(
            lambda: remote(src, dst, fs.at[k], fr.at[here], s, c1, r1).wait_send())

    def sent_edge(c1, r1, k, me):
        src, dst = edge_copy(c1, r1)
        s1 = s + edge_step(c1)
        gone = (s1 >= 0) & (s1 < n_src) if c1 == r1 else jnp.logical_not(me)
        pl.when(gone)(lambda: remote(src, dst, es.at[k], er.at[here], s, c1, r1).wait_send())

    def sent_mask(c1, r1, k, me):
        owner = c == (2 * s) // n_src
        pl.when(owner & jnp.logical_not(me))(
            lambda: remote(m_ref.at[k], mbuf.at[r], ms.at[k], mr.at[r], s, c1, r1).wait_send())

    def sent_out(s1, r1, k, src, me):
        pl.when(jnp.logical_not(me))(
            lambda: remote(src, obuf.at[slot], os.at[k], orr.at[slot], s1, c2, r1).wait_send())

    each(sent_main)
    each(sent_edge)
    each(sent_mask)
    outgoing(sent_out)
    for k in range(1, n_src):
        pz(k).wait_send()
        wz(k).wait_send()
        share_copy(k).wait_send()


def by_pixel(
    features, layout, conv_weight, conv_bias, head_weight, transmission, point_weight, assignment
):
    n_src, n_chan, n_row = (lax.axis_size(a) for a in ("src", "chan", "row"))
    s = lax.axis_index("src")
    layers = conv_weight.shape[1]
    halo = 2**layers - 1
    part, strip, block = features.shape
    ch = part * n_chan
    width = block * n_src
    rows = strip * n_row // 2
    own = block // (n_chan * n_row)
    lanes = 2 * ch
    d_last = 2 ** (layers - 1)
    pairs = features.reshape(part, strip // 2, 2, block // 2, 2).transpose(3, 1, 4, 2, 0)
    pairs = pairs.reshape(block // 2, strip // 2, lanes)
    w = conv_weight[0].reshape(layers, 3, 3, ch, ch)
    zero = jnp.zeros((layers, ch, ch), w.dtype)
    packed = [jnp.concatenate([w[:, 1, b], w[:, 0, b]], -1) for b in range(3)]
    packed.append(jnp.concatenate([w[:, 2, 0], w[:, 2, 1]], -1))
    packed.append(jnp.concatenate([w[:, 2, 2], zero], -1))
    packed = jnp.stack(packed, 1).reshape(2, layers // 2 * 5, ch, lanes)
    planes2 = head_weight.shape[2]
    head = jnp.concatenate(
        [
            head_weight[0].T.astype(jnp.float32),
            jnp.broadcast_to(transmission[0][:, None], (planes2, ch)),
        ],
        1,
    )
    bias = jnp.concatenate([conv_bias[0], conv_bias[0]], 1)
    params = jnp.concatenate([head, bias, jnp.zeros((-layers % 8, lanes), jnp.float32)], 0)
    half_tile = layout.shape[1] // block
    mask = lax.dynamic_slice_in_dim(layout, (s % half_tile) * block, block, 1).astype(jnp.float32)
    mask = mask.reshape(strip // (2 * d_last), 2, d_last, 4, own).transpose(3, 0, 1, 2, 4)
    mask = mask.reshape(4, strip // d_last, d_last * own)
    spec = lambda shape, kind=jnp.bfloat16: pltpu.VMEM(shape, kind)
    scratch = []
    n = own + 2 * halo
    for l in range(layers):
        scratch.append(spec((n, rows, 2 * lanes)))
        n -= 2 * 2**l
    scratch.append(spec((n * rows, lanes), jnp.float32))
    groups = rows // d_last
    scratch += [
        spec((4, block // 4, rows // 2, lanes)),
        spec((n_src,) + packed.shape),
        spec((n_src,) + params.shape, jnp.float32),
        spec((2,) + mask.shape[1:], jnp.float32),
        spec((layers, 16 * ch, 2 * lanes)),
        spec((groups, planes2, own * d_last), jnp.float32),
        spec((2 * n_src, planes2 // 2, own * d_last), jnp.float32),
    ]
    dma = pltpu.SemaphoreType.DMA
    for count in (4, 4, 4, 4, n_src, n_src, n_src, n_src, n_src, n_src, 4, 2, 2 * n_src, 2 * n_src):
        scratch.append(dma((count,)))
    scratch += [dma(()), dma(())]
    vmem = pl.BlockSpec(memory_space=pltpu.VMEM)
    out = pl.pallas_call(
        functools.partial(pixel_kernel, layers, n_src, width),
        out_shape=jax.ShapeDtypeStruct((planes2 // 2, d_last, width // n_chan), jnp.float32),
        in_specs=[vmem] * 6,
        out_specs=vmem,
        scratch_shapes=scratch,
        compiler_params=pltpu.CompilerParams(
            vmem_limit_bytes=56 * 2**20, collective_id=0, has_side_effects=True),
    )(pairs, packed, params, mask, point_weight[None], assignment.reshape(1, -1))
    return out[:, None]


def solution(mesh):
    in_specs = (
        P("chan", ("grp", "row"), "src"),
        P(("grp", "row"), "chan"),
        P("src", None, None, None, None),
        P("src", None, None),
        P("src", None, None),
        P("src", None),
        P(),
        P(),
    )
    out_specs = P(None, ("grp", "row"), "src", "chan")

    def shards(*args):
        features, weights = args[0], args[2]
        halo = 2 ** weights.shape[1] - 1
        own = features.shape[2] // (mesh.shape["chan"] * mesh.shape["row"])
        fits = own >= 2 * halo and mesh.shape["chan"] == mesh.shape["row"] == 2
        body = by_pixel if fits and mesh.shape["src"] == 4 else by_cluster
        return body(*args)

    return jax.shard_map(shards, mesh=mesh, in_specs=in_specs, out_specs=out_specs, check_vma=False)
```

profile of v0, /device:TPU:0, one launch (start us, length us, event | category | flops | bytes accessed | tf_op | source)
XLA Modules:
  0.0 46.6 jit_solution(9193992663508928403)
XLA Ops:
  0.0 1.5 %copy.21 = bf16[32,32,128]{0,2,1:T(8,128)(2,1)S(1)} copy(bf16[32,32,128]{2,1,0:T(8,128)(2,1)} %param.8) | data formatting | bytes 524288 | tf_op args[0]
  1.5 0.7 %copy.22 = bf16[64,16,2,2,32]{0,4,3,2,1:T(8,128)(2,1)S(1)} copy(bf16[64,16,2,2,32]{4,2,0,3,1:T(2,128)(2,1)S(1)} %bitcast.77) | data formatting | bytes 524288 | tf_op jit(solution)/shard_map/transpose | solution.py:460
  2.2 0.0 copy-start
  2.2 1.0 %copy.33.t_ref = bf16[64,16,128]{2,1,0:T(8,128)(2,1)} copy(bf16[64,16,128]{0,2,1:T(8,128)(2,1)S(1)} %bitcast.78) | data formatting | bytes 524288 | tf_op jit(solution)/shard_map/reshape | solution.py:461
  3.2 0.1 copy-done
  3.3 0.1 fusion
  3.4 0.1 fusion.1
  3.5 0.1 fusion.2
  3.6 0.1 fusion.3
  3.8 0.0 copy-start.1
  3.8 0.0 copy-start.5
  3.8 0.7 %copy-done.5 = f32[1,16]{1,0:T(1,128)S(1)} copy-done((f32[1,16]{1,0:T(1,128)S(1)}, f32[1,16]{1,0:T(1,128)}, u32[]{:S(2)}) %copy-start.5) | copy-done | bytes 88
  4.5 0.0 copy-start.3
  4.5 0.1 broadcast_in_dim.18
  4.5 0.6 %copy-done.3 = bf16[1,64,16]{1,2,0:T(8,128)(2,1)S(1)} copy-done((bf16[1,64,16]{1,2,0:T(8,128)(2,1)S(1)}, bf16[1,64,16]{1,2,0:T(8,128)(2,1)}, u32[]{:S(2)}) %copy-start.3) | copy-done | bytes 2072
  5.2 0.0 copy-start.4
  5.2 0.1 pad.5.clone
  5.2 0.6 %copy-done.4 = f32[1,4,64]{2,1,0:T(4,128)S(1)} copy-done((f32[1,4,64]{2,1,0:T(4,128)S(1)}, f32[1,4,64]{2,1,0:T(4,128)}, u32[]{:S(2)}) %copy-start.4) | copy-done | bytes 1048
  5.8 0.0 copy-start.2
  5.8 0.7 %maximum_maximum_fusion.p_ref = f32[24,128]{1,0:T(8,128)} fusion(f32[4,64]{1,0:T(4,128)S(1)} %bitcast.83, f32[16,64]{1,0:T(8,128)S(1)} %broadcast_in_dim.18, f32[16,64]{1,0:T(8,128)S(1)} %convert_bitcast_fusion, f32[24]{0:T(128)S(1)} %pad.5.clone), kind=kLoop, calls=%fused_computation.20 | loop fusion | flops 12288 | bytes 21600 | tf_op jit(solution)/shard_map/concatenate | solution.py:477
  6.5 0.1 copy-done.2
  6.6 0.1 reshape.24
  6.7 0.7 %reshape.25.m_ref = f32[4,4,256]{2,1,0:T(4,128)} reshape(f32[4,2,2,8,32]{4,3,2,1,0:T(8,128)S(1)} %bitcast.81) | data formatting | bytes 32768 | tf_op jit(solution)/shard_map/reshape | solution.py:481
  7.4 0.0 copy-done.1
  7.4 37.7 %shard_map.82 = f32[8,8,256]{2,1,0:T(8,128)} custom-call(bf16[64,16,128]{2,1,0:T(8,128)(2,1)} %copy.33.t_ref, bf16[2,10,64,128]{3,2,1,0:T(8,128)(2,1)} %bitcast.80, f32[24,128]{1,0:T(8,128)} %maximum_maximum_fusion.p_ref, f32[4,4,256]{2,1,0:T(4,128)} %reshape.25.m_ref, f32[1,128]{1,0:T(1,128)} %bitcast.85, s32[1,128]{1,0:T(1,128)} %bitcast.86), custom_call_target="tpu_custom_call" | custom-call | tf_op jit(solution)/shard_map/pallas_call | solution.py:504
  45.2 1.5 %copy.51 = f32[8,1,8,256]{3,2,1,0:T(8,128)} copy(f32[8,1,8,256]{3,2,1,0:T(8,128)} %bitcast.82) | data formatting | bytes 131072
  (6 shorter events, 0.1 us)
Async XLA Ops:
  2.2 1.1 %copy-start = (bf16[1,4,9,64,64]{4,3,2,1,0:T(8,128)(2,1)S(1)}, bf16[1,4,9,64,64]{4,3,2,1,0:T(8,128)(2,1)}, u32[]{:S(2)}) copy-start(bf16[1,4,9,64,64]{4,3,2,1,0:T(8,128)(2,1)} %param.10) | copy-start | bytes 884740
  3.8 3.6 %copy-start.1 = (bf16[4,5,64,128]{3,2,1,0:T(8,128)(2,1)}, bf16[4,5,64,128]{3,2,1,0:T(8,128)(2,1)S(1)}, u32[]{:S(2)}) copy-start(bf16[4,5,64,128]{3,2,1,0:T(8,128)(2,1)S(1)} %bitcast_dynamic-update-slice_fusion) | copy-start | bytes 983044
  3.8 0.7 %copy-start.5 = (f32[1,16]{1,0:T(1,128)S(1)}, f32[1,16]{1,0:T(1,128)}, u32[]{:S(2)}) copy-start(f32[1,16]{1,0:T(1,128)} %param.13) | copy-start | bytes 196
  4.5 0.7 %copy-start.3 = (bf16[1,64,16]{1,2,0:T(8,128)(2,1)S(1)}, bf16[1,64,16]{1,2,0:T(8,128)(2,1)}, u32[]{:S(2)}) copy-start(bf16[1,64,16]{1,2,0:T(8,128)(2,1)} %param.12) | copy-start | bytes 6148
  5.2 0.7 %copy-start.4 = (f32[1,4,64]{2,1,0:T(4,128)S(1)}, f32[1,4,64]{2,1,0:T(4,128)}, u32[]{:S(2)}) copy-start(f32[1,4,64]{2,1,0:T(4,128)} %param.11) | copy-start | bytes 3076
  5.8 0.8 %copy-start.2 = (s32[32,256]{1,0:T(8,128)S(1)}, s32[32,256]{1,0:T(8,128)}, u32[]{:S(2)}) copy-start(s32[32,256]{1,0:T(8,128)} %param.9) | copy-start | bytes 98308
where the time goes:
time: 47 us; the launch traced here: 46.6 us
  Pallas kernels  37.7 us (80%)
  local copies, waits for them, and re-layouts  7.7 us (16%)
  other arithmetic  1.1 us (2%)
    pallas_call x1, Pallas kernels, by_pixel(): pl.pallas_call(functools.partial(pixel_kernel, layers, n_src, width), out...  37.7 us
    unnamed x14, local copies, waits for them, and re-layouts  5.02 us
    reshape x1, local copies, waits for them, and re-layouts, by_pixel(): pairs = pairs.reshape(block // 2, strip // 2, lanes)  0.97 us

commit v1 on v0

--- a/solution.py
+++ b/solution.py
@@ -73,18 +73,30 @@
     return summed[:, None]
 
 
-def gelu(v):
-    c = math.sqrt(2.0 / math.pi)
-    return 0.5 * v * (1.0 + jnp.tanh(v * (c + (c * 0.044715) * (v * v))))
+def gelu_of_half(v):
+    c = 2.0 * math.sqrt(2.0 / math.pi)
+    return v + v * jnp.tanh(v * (c + (c * 4.0 * 0.044715) * (v * v)))
 
 
 def beside(h, d):
-    n = h.shape[1]
-    sub = lax.broadcasted_iota(jnp.int32, h.shape, 1)
-    low = lax.broadcasted_iota(jnp.int32, h.shape, 2) < h.shape[2] // 2
-    rolled = jnp.where(low, pltpu.roll(h, n - d, 1), pltpu.roll(h, d, 1))
-    keep = jnp.where(low, sub, n - 1 - sub) < n - d
-    return jnp.where(keep, rolled, 0.0)
+    n, rows, lanes = h.shape
+    zero = jnp.zeros((n, 8, lanes), h.dtype)
+    tiles = [h[:, 8 * g : 8 * g + 8] for g in range(rows // 8)]
+    low = lax.broadcasted_iota(jnp.int32, zero.shape, 2) < lanes // 2
+    if d % 8 == 0:
+        up = tiles[d // 8 :] + [zero] * (d // 8)
+        down = [zero] * (d // 8) + tiles[: -(d // 8)]
+        return jnp.concatenate([jnp.where(low, a, b) for a, b in zip(up, down)], axis=1)
+    sub = lax.broadcasted_iota(jnp.int32, zero.shape, 1)
+    inner = jnp.where(low, sub, 7 - sub) < 8 - d
+    up = [pltpu.roll(v, 8 - d, 1) for v in tiles] + [zero]
+    down = [zero] + [pltpu.roll(v, d, 1) for v in tiles]
+    out = []
+    for g in range(len(tiles)):
+        near = jnp.where(low, up[g], down[g + 1])
+        far = jnp.where(low, up[g + 1], down[g])
+        out.append(jnp.where(inner, near, far))
+    return jnp.concatenate(out, axis=1)
 
 
 def repair(h, d):
@@ -120,11 +132,11 @@
 
 
 def pixel_kernel(
-    layers, n_src, width, t_ref, w_ref, p_ref, m_ref, pw_ref, as_ref, o_ref, *scratch
+    layers, n_src, t_ref, w_ref, h_ref, tr_ref, b_ref, m_ref, pw_ref, as_ref, o_ref, *scratch
 ):
     bufs = scratch[: layers + 1]
     got, wraw, pbuf, mbuf, wide, acc, obuf = scratch[layers + 1 : layers + 8]
-    fs, fr, es, er, ws, wr, vs, vr, ps, pr, ms, mr, os, orr, lw, lp = scratch[layers + 8 :]
+    fs, fr, es, er, ws, wr, vs, vr, ps, pr, ms, mr, os, orr, lw = scratch[layers + 8 :]
     s, c, r = (lax.axis_index(a) for a in ("src", "chan", "row"))
     halo = 2**layers - 1
     lanes = t_ref.shape[2]
@@ -133,6 +145,16 @@
     piece = t_ref.shape[0] // 8
     here = 2 * c + r
     side = c
+
+    ch = lanes // 2
+    planes2 = h_ref.shape[0]
+    ia = lax.broadcasted_iota(jnp.int32, (planes2, planes2), 0)
+    ib = lax.broadcasted_iota(jnp.int32, (planes2, planes2), 1)
+    column = jnp.sum(jnp.where(ia == ib, tr_ref[...], 0.0), axis=1, keepdims=True)
+    pbuf[0, :planes2, :] = jnp.concatenate(
+        [h_ref[...].astype(jnp.float32), jnp.broadcast_to(column, (planes2, ch))], axis=1)
+    bias_half = 0.5 * b_ref[...]
+    pbuf[0, planes2 : planes2 + layers, :] = jnp.concatenate([bias_half, bias_half], axis=1)
 
     barrier = pltpu.get_barrier_semaphore()
     for s1 in range(n_src):
@@ -203,16 +225,14 @@
         return remote(w_ref.at[r], wraw.at[k, r], ws.at[k], wr.at[k], xor(s, k), c, r)
 
     def pz(k):
-        return remote(p_ref, pbuf.at[k], ps.at[k], pr.at[k], xor(s, k), c, r)
+        return remote(pbuf.at[0], pbuf.at[k], ps.at[k], pr.at[k], xor(s, k), c, r)
 
     for k in range(1, n_src):
         pz(k).start()
         wz(k).start()
     each(send_mask)
     own_w = pltpu.make_async_copy(w_ref, wraw.at[0], lw)
-    own_p = pltpu.make_async_copy(p_ref, pbuf.at[0], lp)
     own_w.start()
-    own_p.start()
 
     wide[...] = jnp.zeros_like(wide)
     outside = ((here == 0) & (s == 0)) | ((here == 3) & (s == n_src - 1))
@@ -222,13 +242,11 @@
         for k in range(4):
             got[k, pl.ds(piece * 3 * side, piece)] = jnp.zeros((piece,) + got.shape[2:], got.dtype)
 
-    ch = lanes // 2
-
     def build(k):
         low = lax.broadcasted_iota(jnp.int32, (ch, lanes), 1) < ch
         per = layers // 2
         for l in range(layers):
-            raw = lambda i: wraw[k, l // per, (l % per) * 5 + i].astype(jnp.float32)
+            raw = lambda i: wraw[k, l // per, (l % per) * 5 + i].astype(jnp.float32) * 0.5
             firsts = [raw(b) for b in range(3)]
             q0, q1 = raw(3), raw(4)
             seconds = [q0, pltpu.roll(q0, ch, 1), q1]
@@ -248,7 +266,6 @@
                         wide[l, at : at + ch, ic * lanes : (ic + 1) * lanes] = v
 
     own_w.wait()
-    own_p.wait()
     build(0)
 
     def wait_main(c1, r1, k, me):
@@ -293,7 +310,8 @@
     bufs[0][:, :, lanes:] = beside(x, 1).astype(jnp.bfloat16)
 
     own_cols = n_in - 2 * halo
-    start = (4 * s + here) * own_cols
+    at_left = (here == 0) & (s == 0)
+    at_right = (here == 3) & (s == n_src - 1)
     for r1 in range(2):
         for_self = (c == (2 * s) // n_src) & (r == r1)
         pl.when(jnp.logical_not(for_self))(
@@ -337,10 +355,17 @@
                 z = jnp.concatenate(parts, axis=0) + bias[None]
                 n = per * 2 * d
                 centre = src[base + d : base + d + n, :, :lanes].astype(jnp.float32)
-                h = centre + gelu(z)
-                col = lax.broadcasted_iota(jnp.int32, h.shape, 0) + (start - halo + margin + base)
-                h = jnp.where((col >= 0) & (col < width), h, 0.0)
-                h = h.astype(jnp.bfloat16).astype(jnp.float32)
+                h = centre + gelu_of_half(z)
+                edge = halo - margin
+                left = min(max(edge - base, 0), n)
+                right = min(max(base + n - (n_out - edge), 0), n - left)
+                if left or right:
+                    cut = [h[left : n - right]]
+                    if left:
+                        cut.insert(0, jnp.where(at_left, 0.0, h[:left]))
+                    if right:
+                        cut.append(jnp.where(at_right, 0.0, h[n - right :]))
+                    h = jnp.concatenate(cut, axis=0)
                 if l + 1 < layers:
                     h = repair(h, d)
                     bufs[l + 1][base : base + n, :, :lanes] = h.astype(jnp.bfloat16)
@@ -466,15 +491,6 @@
     packed.append(jnp.concatenate([w[:, 2, 2], zero], -1))
     packed = jnp.stack(packed, 1).reshape(2, layers // 2 * 5, ch, lanes)
     planes2 = head_weight.shape[2]
-    head = jnp.concatenate(
-        [
-            head_weight[0].T.astype(jnp.float32),
-            jnp.broadcast_to(transmission[0][:, None], (planes2, ch)),
-        ],
-        1,
-    )
-    bias = jnp.concatenate([conv_bias[0], conv_bias[0]], 1)
-    params = jnp.concatenate([head, bias, jnp.zeros((-layers % 8, lanes), jnp.float32)], 0)
     half_tile = layout.shape[1] // block
     mask = lax.dynamic_slice_in_dim(layout, (s % half_tile) * block, block, 1).astype(jnp.float32)
     mask = mask.reshape(strip // (2 * d_last), 2, d_last, 4, own).transpose(3, 0, 1, 2, 4)
@@ -490,7 +506,7 @@
     scratch += [
         spec((4, block // 4, rows // 2, lanes)),
         spec((n_src,) + packed.shape),
-        spec((n_src,) + params.shape, jnp.float32),
+        spec((n_src, planes2 + (layers + 7) // 8 * 8, lanes), jnp.float32),
         spec((2,) + mask.shape[1:], jnp.float32),
         spec((layers, 16 * ch, 2 * lanes)),
         spec((groups, planes2, own * d_last), jnp.float32),
@@ -499,17 +515,17 @@
     dma = pltpu.SemaphoreType.DMA
     for count in (4, 4, 4, 4, n_src, n_src, n_src, n_src, n_src, n_src, 4, 2, 2 * n_src, 2 * n_src):
         scratch.append(dma((count,)))
-    scratch += [dma(()), dma(())]
+    scratch += [dma(())]
     vmem = pl.BlockSpec(memory_space=pltpu.VMEM)
     out = pl.pallas_call(
-        functools.partial(pixel_kernel, layers, n_src, width),
+        functools.partial(pixel_kernel, layers, n_src),
         out_shape=jax.ShapeDtypeStruct((planes2 // 2, d_last, width // n_chan), jnp.float32),
-        in_specs=[vmem] * 6,
+        in_specs=[vmem] * 8,
         out_specs=vmem,
         scratch_shapes=scratch,
         compiler_params=pltpu.CompilerParams(
             vmem_limit_bytes=56 * 2**20, collective_id=0, has_side_effects=True),
-    )(pairs, packed, params, mask, point_weight[None], assignment.reshape(1, -1))
+    )(pairs, packed, head_weight[0].T, transmission, conv_bias[0], mask, point_weight[None], assignment.reshape(1, -1))
     return out[:, None]
 
 

time: 47 us -> 43.4 us (0.923)
  Pallas kernels: 37.7 us -> 36.2 us
  local copies, waits for them, and re-layouts: 7.7 us -> 6.34 us
  other arithmetic: 1.1 us -> 0.42 us
    pallas_call x1, Pallas kernels: 37.7 us -> 36.2 us  [by_pixel(): pl.pallas_call(functools.partial(pixel_kernel, layers, n_src), out_shape=...]
    unnamed x14 -> x8, local copies, waits for them, and re-layouts: 5.02 us -> 3.81 us
    concatenate x1 -> x0, other arithmetic: 0.67 us -> none  [by_pixel(): jnp.concatenate([head, bias, jnp.zeros((-layers % 8, lanes), jnp.float32)...]
where the time goes in v1:
time: 43.4 us; the launch traced here: 43 us
  Pallas kernels  36.2 us (83%)
  local copies, waits for them, and re-layouts  6.34 us (15%)
    pallas_call x1, Pallas kernels, by_pixel(): pl.pallas_call(functools.partial(pixel_kernel, layers, n_src), out_shape=...  36.2 us
    unnamed x8, local copies, waits for them, and re-layouts  3.81 us
    reshape x1, local copies, waits for them, and re-layouts, by_pixel(): pairs = pairs.reshape(block // 2, strip // 2, lanes)  0.96 us

profile of v1, /device:TPU:0, one launch (start us, length us, event | category | flops | bytes accessed | tf_op | source)
XLA Modules:
  0.0 43.0 jit_solution(11444563368850297653)
XLA Ops:
  0.0 1.5 %copy.21 = bf16[32,32,128]{0,2,1:T(8,128)(2,1)S(1)} copy(bf16[32,32,128]{2,1,0:T(8,128)(2,1)} %param.8) | data formatting | bytes 524288 | tf_op args[0]
  1.5 0.7 %copy.22 = bf16[64,16,2,2,32]{0,4,3,2,1:T(8,128)(2,1)S(1)} copy(bf16[64,16,2,2,32]{4,2,0,3,1:T(2,128)(2,1)S(1)} %bitcast.74) | data formatting | bytes 524288 | tf_op jit(solution)/shard_map/transpose | solution.py:485
  2.2 0.0 copy-start
  2.2 1.0 %copy.33.t_ref = bf16[64,16,128]{2,1,0:T(8,128)(2,1)} copy(bf16[64,16,128]{0,2,1:T(8,128)(2,1)S(1)} %bitcast.75) | data formatting | bytes 524288 | tf_op jit(solution)/shard_map/reshape | solution.py:486
  3.2 0.1 copy-done
  3.3 0.1 fusion
  3.4 0.1 fusion.1
  3.5 0.1 fusion.2
  3.6 0.1 fusion.3
  3.8 0.0 copy-start.1
  3.8 0.0 copy-start.2
  3.8 0.8 %copy-done.2 = s32[32,256]{1,0:T(8,128)S(1)} copy-done((s32[32,256]{1,0:T(8,128)S(1)}, s32[32,256]{1,0:T(8,128)}, u32[]{:S(2)}) %copy-start.2) | copy-done | bytes 32792
  4.6 0.1 reshape.21
  4.7 0.7 %reshape.22.m_ref = f32[4,4,256]{2,1,0:T(4,128)} reshape(f32[4,2,2,8,32]{4,3,2,1,0:T(8,128)S(1)} %bitcast.79) | data formatting | bytes 32768 | tf_op jit(solution)/shard_map/reshape | solution.py:497
  5.4 0.0 copy-done.1
  5.4 36.2 %shard_map.82 = f32[8,8,256]{2,1,0:T(8,128)} custom-call(bf16[64,16,128]{2,1,0:T(8,128)(2,1)} %copy.33.t_ref, bf16[2,10,64,128]{3,2,1,0:T(8,128)(2,1)} %bitcast.77, bf16[16,64]{1,0:T(8,128)(2,1)} %bitcast.80, f32[1,16]{1,0:T(1,128)} %tr_ref.1, f32[4,64]{1,0:T(4,128)} %bitcast.81, f32[4,4,256]{2,1,0:T(4,128)} %reshape.22.m_ref, f32[1,128]{1,0:T(1,128)} %bitcast.82, ...), custom_call_target="tpu_custom_call" | custom-call | tf_op jit(solution)/shard_map/pallas_call | solution.py:520
  41.6 1.5 %copy.51 = f32[8,1,8,256]{3,2,1,0:T(8,128)} copy(f32[8,1,8,256]{3,2,1,0:T(8,128)} %bitcast.78) | data formatting | bytes 131072
  (4 shorter events, 0.1 us)
Async XLA Ops:
  2.2 1.1 %copy-start = (bf16[1,4,9,64,64]{4,3,2,1,0:T(8,128)(2,1)S(1)}, bf16[1,4,9,64,64]{4,3,2,1,0:T(8,128)(2,1)}, u32[]{:S(2)}) copy-start(bf16[1,4,9,64,64]{4,3,2,1,0:T(8,128)(2,1)} %param.10) | copy-start | bytes 884740
  3.8 1.6 %copy-start.1 = (bf16[4,5,64,128]{3,2,1,0:T(8,128)(2,1)}, bf16[4,5,64,128]{3,2,1,0:T(8,128)(2,1)S(1)}, u32[]{:S(2)}) copy-start(bf16[4,5,64,128]{3,2,1,0:T(8,128)(2,1)S(1)} %bitcast_dynamic-update-slice_fusion) | copy-start | bytes 983044
  3.8 0.8 %copy-start.2 = (s32[32,256]{1,0:T(8,128)S(1)}, s32[32,256]{1,0:T(8,128)}, u32[]{:S(2)}) copy-start(s32[32,256]{1,0:T(8,128)} %param.9) | copy-start | bytes 98308

commit v2 on v1

--- a/solution.py
+++ b/solution.py
@@ -334,6 +334,9 @@
             margin += d
             groups = n_out // (2 * d)
             per = chunks_of(groups, d, rows)
+            if l == layers - 2 and k + 1 < n_src:
+                wz(k + 1).wait_recv()
+                share_copy(k + 1).start()
             bias = pbuf[k, 2 * q2 + l : 2 * q2 + l + 1, :]
             for chunk in range(groups // per):
                 base = chunk * per * 2 * d
@@ -398,9 +401,6 @@
 
     q2 = acc.shape[1] // 2
     for k in range(n_src):
-        if k + 1 < n_src:
-            wz(k + 1).wait_recv()
-            share_copy(k + 1).start()
         if k > 0:
             remote(
                 wraw.at[k, 1 - r], wraw.at[k, 1 - r], vs.at[k], vr.at[k], s, c, 1 - r

time: 43.4 us -> 42.9 us (0.988)
  Pallas kernels: 36.2 us -> 35.7 us
    pallas_call x1, Pallas kernels: 36.2 us -> 35.7 us  [by_pixel(): pl.pallas_call(functools.partial(pixel_kernel, layers, n_src), out_shape=...]
where the time goes in v2:
time: 42.9 us; the launch traced here: 42.5 us
  Pallas kernels  35.7 us (83%)
  local copies, waits for them, and re-layouts  6.34 us (15%)
    pallas_call x1, Pallas kernels, by_pixel(): pl.pallas_call(functools.partial(pixel_kernel, layers, n_src), out_shape=...  35.7 us
    unnamed x8, local copies, waits for them, and re-layouts  3.81 us
    reshape x1, local copies, waits for them, and re-layouts, by_pixel(): pairs = pairs.reshape(block // 2, strip // 2, lanes)  0.96 us

profile of v2, /device:TPU:0, one launch (start us, length us, event | category | flops | bytes accessed | tf_op | source)
XLA Modules:
  0.0 42.5 jit_solution(15367461729884013127)
XLA Ops:
  0.0 1.5 %copy.21 = bf16[32,32,128]{0,2,1:T(8,128)(2,1)S(1)} copy(bf16[32,32,128]{2,1,0:T(8,128)(2,1)} %param.8) | data formatting | bytes 524288 | tf_op args[0]
  1.5 0.7 %copy.22 = bf16[64,16,2,2,32]{0,4,3,2,1:T(8,128)(2,1)S(1)} copy(bf16[64,16,2,2,32]{4,2,0,3,1:T(2,128)(2,1)S(1)} %bitcast.74) | data formatting | bytes 524288 | tf_op jit(solution)/shard_map/transpose | solution.py:485
  2.2 0.0 copy-start
  2.2 1.0 %copy.33.t_ref = bf16[64,16,128]{2,1,0:T(8,128)(2,1)} copy(bf16[64,16,128]{0,2,1:T(8,128)(2,1)S(1)} %bitcast.75) | data formatting | bytes 524288 | tf_op jit(solution)/shard_map/reshape | solution.py:486
  3.2 0.1 copy-done
  3.3 0.1 fusion
  3.4 0.1 fusion.1
  3.5 0.1 fusion.2
  3.6 0.1 fusion.3
  3.8 0.0 copy-start.1
  3.8 0.0 copy-start.2
  3.8 0.8 %copy-done.2 = s32[32,256]{1,0:T(8,128)S(1)} copy-done((s32[32,256]{1,0:T(8,128)S(1)}, s32[32,256]{1,0:T(8,128)}, u32[]{:S(2)}) %copy-start.2) | copy-done | bytes 32792
  4.6 0.1 reshape.21
  4.7 0.7 %reshape.22.m_ref = f32[4,4,256]{2,1,0:T(4,128)} reshape(f32[4,2,2,8,32]{4,3,2,1,0:T(8,128)S(1)} %bitcast.79) | data formatting | bytes 32768 | tf_op jit(solution)/shard_map/reshape | solution.py:497
  5.4 0.0 copy-done.1
  5.4 35.7 %shard_map.82 = f32[8,8,256]{2,1,0:T(8,128)} custom-call(bf16[64,16,128]{2,1,0:T(8,128)(2,1)} %copy.33.t_ref, bf16[2,10,64,128]{3,2,1,0:T(8,128)(2,1)} %bitcast.77, bf16[16,64]{1,0:T(8,128)(2,1)} %bitcast.80, f32[1,16]{1,0:T(1,128)} %tr_ref.1, f32[4,64]{1,0:T(4,128)} %bitcast.81, f32[4,4,256]{2,1,0:T(4,128)} %reshape.22.m_ref, f32[1,128]{1,0:T(1,128)} %bitcast.82, ...), custom_call_target="tpu_custom_call" | custom-call | tf_op jit(solution)/shard_map/pallas_call | solution.py:520
  41.1 1.5 %copy.51 = f32[8,1,8,256]{3,2,1,0:T(8,128)} copy(f32[8,1,8,256]{3,2,1,0:T(8,128)} %bitcast.78) | data formatting | bytes 131072
  (4 shorter events, 0.1 us)
Async XLA Ops:
  2.2 1.1 %copy-start = (bf16[1,4,9,64,64]{4,3,2,1,0:T(8,128)(2,1)S(1)}, bf16[1,4,9,64,64]{4,3,2,1,0:T(8,128)(2,1)}, u32[]{:S(2)}) copy-start(bf16[1,4,9,64,64]{4,3,2,1,0:T(8,128)(2,1)} %param.10) | copy-start | bytes 884740
  3.8 1.6 %copy-start.1 = (bf16[4,5,64,128]{3,2,1,0:T(8,128)(2,1)}, bf16[4,5,64,128]{3,2,1,0:T(8,128)(2,1)S(1)}, u32[]{:S(2)}) copy-start(bf16[4,5,64,128]{3,2,1,0:T(8,128)(2,1)S(1)} %bitcast_dynamic-update-slice_fusion) | copy-start | bytes 983044
  3.8 0.8 %copy-start.2 = (s32[32,256]{1,0:T(8,128)S(1)}, s32[32,256]{1,0:T(8,128)}, u32[]{:S(2)}) copy-start(s32[32,256]{1,0:T(8,128)} %param.9) | copy-start | bytes 98308
